TPU v7x, 512 devices: a whole 4x4x16 slice. The times are simulated.
512 devices in a mesh: vol: 8 (over y, core), surf: 64 (over x, z).
Axes of the slice: x: 4, y: 4, z: 16, core: 2. Of those that a mesh axis runs over, the one named last changes fastest.
Arguments:
- vol_coords: float32 [3, 32768], P(None, 'vol'), may hold values from 0 to 64, as said below
- surf_coords: float32 [3, 65536], P(None, 'surf'), may hold values from 0 to 64, as said below
- vol_sens: bfloat16 [96, 32768], P(None, 'vol'), may hold values from -6 to 6
- links: int32 [8, 65536], P(None, 'surf'), may hold values from -1 to 65535, as said below
Outputs:
- smooth_sens: float32 [96, 65536], P('vol', 'surf')
Inputs may be any that keep to these rules, and one draw needn't show every extreme that they name: `vol_coords`: row 0 is a node's span position in patch widths, within 0 to 64; row 1 its chordwise position, within 0 to 1; row 2 its height above the surface, within 0.005 to 2. `surf_coords`: surface node i belongs to patch i // 1024; row 0 of a node of patch p lies within p to p + 1, row 1 within 0 to 1, row 2 within 0 to 0.02. `links`: each valid entry of node i names a surface node of i's patch or of one of the two patches beside it on the cycle of 64 patches (patch indices taken mod 64); slot 0 is always valid, and the valid slots of a node come before its empty ones.
All inputs are finite; a program needn't handle non-finite values.
Results may differ from a plain program's by a relative error of at most 0.0003.
Values sent between devices are 32-bit elements; how exact they have to be, the bound alone decides.
A program may use at most 64 MiB of HBM per device.

v0:
```python
import jax
import jax.numpy as jnp
from jax import lax
from jax.sharding import PartitionSpec as P

SWEEPS = 4


near_square = 0.0016
far_square = 4.0
far_weight = 0.001
smoothing = 2.0


def with_halo(value, sides, width):
    for axis, dim in sides:
        size, length = (lax.axis_size(axis), value.shape[dim])
        up = [(i, (i + 1) % size) for i in range(size)]
        down = [(j, i) for i, j in up]
        last = lax.slice_in_dim(value, length - width, length, axis=dim)
        initial = lax.slice_in_dim(value, 0, width, axis=dim)
        before = lax.ppermute(last, axis, up)
        after = lax.ppermute(initial, axis, down)
        value = jnp.concatenate([before, value, after], axis=dim)
    return value


def idw_weights(vol_block, surf_block):
    delta = vol_block[0][:, None] - surf_block[0][None, :]
    dist_sq = delta * delta
    delta = vol_block[1][:, None] - surf_block[1][None, :]
    dist_sq = dist_sq + delta * delta
    delta = vol_block[2][:, None] - surf_block[2][None, :]
    dist_sq = dist_sq + delta * delta
    near = near_square / (dist_sq + near_square)
    return near * near + far_weight * far_square / (dist_sq + far_square)


def relax(region, index, valid, rhs, degree):
    total = jnp.zeros(rhs.shape, jnp.float32)
    for slot in range(index.shape[0]):
        picked = jnp.take(region, index[slot], axis=1)
        total = total + jnp.where(valid[slot][None, :], picked, jnp.float32(0.0))
    return (rhs + smoothing * total) / (1.0 + smoothing * degree[None, :])


def local_index(link_block, reach, patch_size):
    patches = lax.axis_size("surf")
    centre = lax.axis_index("surf")
    valid = link_block >= 0
    safe = jnp.maximum(link_block, 0)
    relative = (safe // patch_size - centre + reach + patches) % patches
    index = relative * patch_size + safe % patch_size
    degree = jnp.sum(valid.astype(jnp.float32), axis=0)
    return (index, valid, degree)


def per_device(vol_coords, surf_coords, vol_sens, links):
    vol_count = vol_coords.shape[1]
    patch_size = surf_coords.shape[1]
    rows = vol_sens.shape[0]
    width = min(1024, vol_count)
    turns = vol_count // width

    def add_totals(turn, totals):
        start = turn * width
        block = lax.dynamic_slice_in_dim(vol_coords, start, width, 1)
        sums = jnp.sum(idw_weights(block, surf_coords), axis=1)
        return lax.dynamic_update_slice_in_dim(totals, sums, start, 0)

    local_totals = lax.fori_loop(0, turns, add_totals, jnp.zeros((vol_count,), jnp.float32))
    totals = lax.psum(local_totals, "surf")
    scaled = vol_sens.astype(jnp.float32) / totals[None, :]

    def add_product(turn, partial_value):
        start = turn * width
        block = lax.dynamic_slice_in_dim(vol_coords, start, width, 1)
        sens_block = lax.dynamic_slice_in_dim(scaled, start, width, 1)
        weights = idw_weights(block, surf_coords)
        return partial_value + jnp.dot(
            sens_block, weights, precision=lax.Precision.HIGHEST, preferred_element_type=jnp.float32
        )

    partial_value = lax.fori_loop(0, turns, add_product, jnp.zeros((rows, patch_size), jnp.float32))
    share = rows // lax.axis_size("vol")
    summed = lax.psum(partial_value, "vol")
    source = lax.dynamic_slice_in_dim(summed, lax.axis_index("vol") * share, share, 0)
    index, valid, degree = local_index(links, 1, patch_size)
    current = source
    for sweep in range(SWEEPS):
        region = with_halo(current, (("surf", 1),), patch_size)
        current = relax(region, index, valid, source, degree)
    return current


def solution(mesh):
    return jax.shard_map(
        per_device,
        mesh=mesh,
        in_specs=(P(None, "vol"), P(None, "surf"), P(None, "vol"), P(None, "surf")),
        out_specs=P("vol", "surf"),
        check_vma=False,
    )
```

profile of v0, /device:TPU:24, one launch (start us, length us, event | category | flops | bytes accessed | tf_op | source)
XLA Modules:
  0.0 635.7 jit_solution(7758794114916707139)
XLA Ops:
  6.5 15.9 %while.27 = (s32[]{:T(128)}, f32[4096]{0:T(1024)S(1)}, f32[3,4096]{1,0:T(4,128)}, f32[3,1024]{1,0:T(4,128)}, s32[]{:T(128)}, /*index=5*/s32[]{:T(128)}, s32[]{:T(128)}, s32[]{:T(128)}, s32[]{}, s32[]{}) while((s32[]{:T(128)}, f32[4096]{0:T(1024)S(1)}, f32[3,4096]{1,0:T(4,128)}, f32[3,1024]{1,0:T(4,128)}, s32[]{:T(128)}, /*index=5*/s32[]{:T(128)}, ...), condition=%wide.region_2.0_spmd, body=%wide.region_0.0_spmd.sunk | while | flops 15727624 | bytes 86203 | solution.py:71
  7.5 2.7 add_reduce_fusion.2
  11.5 2.7 add_reduce_fusion.2
  15.5 2.7 add_reduce_fusion.2
  19.4 2.7 add_reduce_fusion.2
  22.5 285.7 %psum.14 = f32[4096]{0:T(1024)S(1)} all-reduce(f32[4096]{0:T(1024)S(1)} %get-tuple-element.179), channel_id=1, replica_groups=mesh['vol'=8,'surf'=64] {'surf'}, use_global_device_ids=true, to_apply=%region_3.0 | all-reduce | flops 4096 | bytes 32768 | tf_op jit(solution)/shard_map/psum | solution.py:72
  309.5 23.2 %while.28 = (s32[]{:T(128)}, f32[96,1024]{1,0:T(8,128)S(1)}, f32[96,4096]{1,0:T(8,128)S(1)}, f32[3,4096]{1,0:T(4,128)}, f32[3,1024]{1,0:T(4,128)S(1)}, /*index=5...) while((s32[]{:T(128)}, f32[96,1024]{1,0:T(8,128)S(1)}, ...), condition=%wide.region_5.0_spmd.clone, body=%wide.region_4.0_spmd.clone.sunk | while | flops 1222836224 | bytes 1253589 | solution.py:84
  310.4 4.9 fusion.94
  316.3 4.8 fusion.94
  322.1 4.8 fusion.94
  327.9 4.8 fusion.94
  334.1 62.5 %all-reduce.2.cloned.1.call-done = f32[96,1024]{0,1:T(8,128)} async-done(((f32[96,1024]{0,1:T(8,128)}), f32[96,1024]{0,1:T(8,128)}) %all-reduce.2.cloned.1.call-update) | async-done | bytes 393232 | tf_op jit(solution)/shard_map/psum | solution.py:86
  397.9 8.1 %collective-permute-start.1 = (f32[12,1024]{0,1:T(8,128)S(1)}, f32[12,1024]{0,1:T(8,128)S(1)}, u32[]{:S(2)}, u32[]{:S(2)}) collective-permute-start(f32[12,1024]{0,1:T(8,128)S(1)} %constant_dynamic-slice_fusion.2), channel_id=1, source_target_pairs={{1,0},{2,1},{3,2},{4,3},{5,4},{6,5},{7,6},{8,7},{9,8},{10,9},{11,1... | collective-permute-start | bytes 147464 | tf_op jit(solution)/shard_map/ppermute | solution.py:23
  406.0 1.9 collective-permute-start
  408.0 10.1 %collective-permute-done.1 = f32[12,1024]{0,1:T(8,128)S(1)} collective-permute-done((f32[12,1024]{0,1:T(8,128)S(1)}, f32[12,1024]{0,1:T(8,128)S(1)}, u32[]{:S(2)}, u32[]{:S(2)}) %collective-permute-start.1) | collective-permute-done | bytes 49184 | tf_op jit(solution)/shard_map/ppermute | solution.py:23
  418.1 7.4 %collective-permute-done = f32[12,1024]{0,1:T(8,128)S(1)} collective-permute-done((f32[12,1024]{0,1:T(8,128)S(1)}, f32[12,1024]{0,1:T(8,128)S(1)}, u32[]{:S(2)}, u32[]{:S(2)}) %collective-permute-start) | collective-permute-done | bytes 49184 | tf_op jit(solution)/shard_map/ppermute | solution.py:22
  425.6 2.8 gather_fusion.7
  428.4 2.8 gather_fusion.6
  431.3 4.0 gather_fusion.5
  435.3 4.0 gather_fusion.4
  439.2 4.0 gather_fusion.3
  443.2 4.0 gather_fusion.2
  447.2 4.0 gather_fusion.1
  451.2 4.0 gather_fusion
  455.2 6.1 fusion.65
  461.3 1.9 collective-permute-start.3
  463.3 3.9 collective-permute-start.2
  467.2 9.5 %collective-permute-done.3 = f32[12,1024]{0,1:T(8,128)S(1)} collective-permute-done((f32[12,1024]{0,1:T(8,128)S(1)}, f32[12,1024]{0,1:T(8,128)S(1)}, u32[]{:S(2)}, u32[]{:S(2)}) %collective-permute-start.3) | collective-permute-done | bytes 49184 | tf_op jit(solution)/shard_map/ppermute | solution.py:23
  476.7 5.2 collective-permute-done.2
  482.1 2.8 gather_fusion.15
  484.9 2.8 gather_fusion.14
  487.7 4.0 gather_fusion.13
  491.7 4.0 gather_fusion.12
  495.7 4.0 gather_fusion.11
  499.7 4.0 gather_fusion.10
  503.7 4.0 gather_fusion.9
  507.6 4.0 gather_fusion.8
  511.6 6.1 fusion.55
  517.8 1.9 collective-permute-start.5
  519.7 4.1 collective-permute-start.4
  523.8 8.5 %collective-permute-done.5 = f32[12,1024]{0,1:T(8,128)S(1)} collective-permute-done((f32[12,1024]{0,1:T(8,128)S(1)}, f32[12,1024]{0,1:T(8,128)S(1)}, u32[]{:S(2)}, u32[]{:S(2)}) %collective-permute-start.5) | collective-permute-done | bytes 49184 | tf_op jit(solution)/shard_map/ppermute | solution.py:23
  532.3 5.2 collective-permute-done.4
  537.6 2.8 gather_fusion.23
  540.4 2.8 gather_fusion.22
  543.3 4.0 gather_fusion.21
  547.3 4.0 gather_fusion.20
  551.3 4.0 gather_fusion.19
  555.2 4.0 gather_fusion.18
  559.2 4.0 gather_fusion.17
  563.2 4.0 gather_fusion.16
  567.2 6.1 fusion.45
  573.3 1.9 collective-permute-start.7
  575.3 3.9 collective-permute-start.6
  579.2 7.8 %collective-permute-done.7 = f32[12,1024]{0,1:T(8,128)S(1)} collective-permute-done((f32[12,1024]{0,1:T(8,128)S(1)}, f32[12,1024]{0,1:T(8,128)S(1)}, u32[]{:S(2)}, u32[]{:S(2)}) %collective-permute-start.7) | collective-permute-done | bytes 49184 | tf_op jit(solution)/shard_map/ppermute | solution.py:23
  587.0 5.2 collective-permute-done.6
  592.3 2.8 gather_fusion.31
  595.2 2.8 gather_fusion.30
  598.0 4.0 gather_fusion.29
  602.0 4.0 gather_fusion.28
  606.0 4.0 gather_fusion.27
  610.0 4.0 gather_fusion.26
  613.9 4.0 gather_fusion.25
  617.9 4.0 gather_fusion.24
  621.9 6.1 fusion.35
  (47 shorter events, 13.8 us)
Async XLA Ops:
  6.5 390.1 %all-reduce.2.cloned.1.call-start = ((), (), s32[]{:S(2)}) async-start(), calls=%async_computation | async-start | bytes 1048576 | tf_op jit(solution)/shard_map/psum | solution.py:86
  22.5 287.0 %copy-start.1 = (f32[3,1024]{1,0:T(4,128)S(1)}, f32[3,1024]{1,0:T(4,128)}, u32[]{:S(2)}) copy-start(f32[3,1024]{1,0:T(4,128)} %get-tuple-element.416) | copy-start | bytes 36868
  309.5 24.3 %copy-start.2 = (s32[8,1024]{1,0:T(8,128)S(1)}, s32[8,1024]{1,0:T(8,128)}, u32[]{:S(2)}) copy-start(s32[8,1024]{1,0:T(8,128)} %param.13) | copy-start | bytes 98308
  397.9 20.2 %collective-permute-start.1 = (f32[12,1024]{0,1:T(8,128)S(1)}, f32[12,1024]{0,1:T(8,128)S(1)}, u32[]{:S(2)}, u32[]{:S(2)}) collective-permute-start(f32[12,1024]{0,1:T(8,128)S(1)} %constant_dynamic-slice_fusion.2), channel_id=1, source_target_pairs={{1,0},{2,1},{3,2},{4,3},{5,4},{6,5},{7,6},{8,7},{9,8},{10,9},{11,1... | collective-permute-start | bytes 147464 | tf_op jit(solution)/shard_map/ppermute | solution.py:23
  406.0 19.6 %collective-permute-start = (f32[12,1024]{0,1:T(8,128)S(1)}, f32[12,1024]{0,1:T(8,128)S(1)}, u32[]{:S(2)}, u32[]{:S(2)}) collective-permute-start(f32[12,1024]{0,1:T(8,128)S(1)} %constant_dynamic-slice_fusion.2), channel_id=1, source_target_pairs={{0,1},{1,2},{2,3},{3,4},{4,5},{5,6},{6,7},{7,8},{8,9},{9,10},{10,1... | collective-permute-start | bytes 147464 | tf_op jit(solution)/shard_map/ppermute | solution.py:22
  435.3 19.9 %copy-start = (f32[96,1024]{0,1:T(8,128)S(1)}, f32[96,1024]{0,1:T(8,128)}, u32[]{:S(2)}) copy-start(f32[96,1024]{0,1:T(8,128)} %all-reduce.2.cloned.1.call-done) | copy-start | bytes 1179652
  461.3 15.4 %collective-permute-start.3 = (f32[12,1024]{0,1:T(8,128)S(1)}, f32[12,1024]{0,1:T(8,128)S(1)}, u32[]{:S(2)}, u32[]{:S(2)}) collective-permute-start(f32[12,1024]{0,1:T(8,128)S(1)} %fusion.65), channel_id=1, source_target_pairs={{1,0},{2,1},{3,2},{4,3},{5,4},{6,5},{7,6},{8,7},{9,8},{10,9},{11,1... | collective-permute-start | bytes 147464 | tf_op jit(solution)/shard_map/ppermute | solution.py:23
  463.3 18.7 %collective-permute-start.2 = (f32[12,1024]{0,1:T(8,128)S(1)}, f32[12,1024]{0,1:T(8,128)S(1)}, u32[]{:S(2)}, u32[]{:S(2)}) collective-permute-start(f32[12,1024]{0,1:T(8,128)S(1)} %fusion.65), channel_id=1, source_target_pairs={{0,1},{1,2},{2,3},{3,4},{4,5},{5,6},{6,7},{7,8},{8,9},{9,10},{10,1... | collective-permute-start | bytes 147464 | tf_op jit(solution)/shard_map/ppermute | solution.py:22
  517.8 14.5 %collective-permute-start.5 = (f32[12,1024]{0,1:T(8,128)S(1)}, f32[12,1024]{0,1:T(8,128)S(1)}, u32[]{:S(2)}, u32[]{:S(2)}) collective-permute-start(f32[12,1024]{0,1:T(8,128)S(1)} %fusion.55), channel_id=1, source_target_pairs={{1,0},{2,1},{3,2},{4,3},{5,4},{6,5},{7,6},{8,7},{9,8},{10,9},{11,1... | collective-permute-start | bytes 147464 | tf_op jit(solution)/shard_map/ppermute | solution.py:23
  519.7 17.8 %collective-permute-start.4 = (f32[12,1024]{0,1:T(8,128)S(1)}, f32[12,1024]{0,1:T(8,128)S(1)}, u32[]{:S(2)}, u32[]{:S(2)}) collective-permute-start(f32[12,1024]{0,1:T(8,128)S(1)} %fusion.55), channel_id=1, source_target_pairs={{0,1},{1,2},{2,3},{3,4},{4,5},{5,6},{6,7},{7,8},{8,9},{9,10},{10,1... | collective-permute-start | bytes 147464 | tf_op jit(solution)/shard_map/ppermute | solution.py:22
  573.3 13.7 %collective-permute-start.7 = (f32[12,1024]{0,1:T(8,128)S(1)}, f32[12,1024]{0,1:T(8,128)S(1)}, u32[]{:S(2)}, u32[]{:S(2)}) collective-permute-start(f32[12,1024]{0,1:T(8,128)S(1)} %fusion.45), channel_id=1, source_target_pairs={{1,0},{2,1},{3,2},{4,3},{5,4},{6,5},{7,6},{8,7},{9,8},{10,9},{11,1... | collective-permute-start | bytes 147464 | tf_op jit(solution)/shard_map/ppermute | solution.py:23
  575.3 17.0 %collective-permute-start.6 = (f32[12,1024]{0,1:T(8,128)S(1)}, f32[12,1024]{0,1:T(8,128)S(1)}, u32[]{:S(2)}, u32[]{:S(2)}) collective-permute-start(f32[12,1024]{0,1:T(8,128)S(1)} %fusion.45), channel_id=1, source_target_pairs={{0,1},{1,2},{2,3},{3,4},{4,5},{5,6},{6,7},{7,8},{8,9},{9,10},{10,1... | collective-permute-start | bytes 147464 | tf_op jit(solution)/shard_map/ppermute | solution.py:22
Sparse Core Ops, SparseCore 0:
  333.9 62.6 all-reduce.1
where the time goes:
time: 638 us; the launch traced here: 636 us
  blocking collectives  286 us (45%)
  local copies, waits for them, and re-layouts  130 us (20%)
  waiting for transfers between devices  122 us (19%)
  other arithmetic  37.3 us (6%)
  starting transfers between devices  27.7 us (4%)
  matrix products  19.4 us (3%)
  between operations  13.8 us (2%)
    psum x1, blocking collectives, per_device(): totals = lax.psum(local_totals, 'surf')  286 us
    gather x32, local copies, waits for them, and re-layouts, relax(): picked = jnp.take(region, index[slot], axis=1)  118 us
    psum x1, waiting for transfers between devices, per_device(): summed = lax.psum(partial_value, 'vol')  62.5 us
    ppermute x4, waiting for transfers between devices, with_halo(): after = lax.ppermute(initial, axis, down)  35.9 us
    div x4, other arithmetic, relax(): return (rhs + smoothing * total) / (1.0 + smoothing * degree[None, :])  24.5 us
    ppermute x4, waiting for transfers between devices, with_halo(): before = lax.ppermute(last, axis, up)  23.2 us
    dot_general x4, matrix products, add_product(): jnp.dot(sens_block, weights, precision=lax.Precision.HIGHEST, preferred_e...  19.4 us
    ppermute x4, starting transfers between devices, with_halo(): before = lax.ppermute(last, axis, up)  13.9 us
  transfers between devices with their start and end apart: 9, of which 9 were waited for; matrix products, arithmetic and copies ran while one was open for 0% of the time, Pallas kernels for 0%

commit v1 on v0

v1 whole, which is shorter than its diff:
```python
import functools

import jax
import jax.numpy as jnp
from jax import lax
from jax.experimental import pallas as pl
from jax.experimental.pallas import tpu as pltpu
from jax.sharding import PartitionSpec as P

SWEEPS = 4
NX, NZ, NY = 4, 16, 4
PATCHES = NX * NZ
LANES = 128
MESH = pl.DeviceIdType.MESH

near_square = 0.0016
far_square = 4.0
far_weight = 0.001
smoothing = 2.0

ROWS_W = 64
ROWS_A = 64
NT = (((1,), (1,)), ((), ()))


def split(value):
    high = value.astype(jnp.bfloat16)
    low = (value - high.astype(jnp.float32)).astype(jnp.bfloat16)
    return high, low


def kernel(
    vol_ref, surf_ref, sens_ref, links_ref, out_ref,
    surf_cols, w_high, w_low, tot, rx, zsend, zbuf, inv, scaled, prod, rs, pr, ysend, yr,
    cur, halo, idx, adj, stage,
    sx_sem, rx_sem, sz_sem, rz_sem, sg_sem, rg_sem, sp_sem, rp_sem, sy_sem, ry_sem, sh_sem, rh_sem,
):
    nv = vol_ref.shape[1]
    ns = surf_ref.shape[1]
    share = out_ref.shape[0]
    vol = lax.axis_index("vol")
    surf = lax.axis_index("surf")
    x, z = surf // NZ, lax.rem(surf, NZ)
    y, core = vol // 2, lax.rem(vol, 2)
    x_peers = [(vol, lax.rem(x + d, NX) * NZ + z) for d in range(1, NX)]
    z_peers = [(vol, x * NZ + lax.rem(z + d, NZ)) for d in range(1, NZ)]
    y_peers = [(lax.rem(y + d, NY) * 2 + core, surf) for d in range(1, NY)]
    partner = (y * 2 + 1 - core, surf)
    right = (vol, lax.rem(surf + 1, PATCHES))
    left = (vol, lax.rem(surf + PATCHES - 1, PATCHES))

    barrier = pltpu.get_barrier_semaphore()
    peers = z_peers + x_peers + y_peers + [partner, left, right]
    for peer in peers:
        pl.semaphore_signal(barrier, inc=1, device_id=peer, device_id_type=MESH)

    def send(src, dst, send_sem, recv_sem, peer):
        copy = pltpu.make_async_remote_copy(
            src_ref=src, dst_ref=dst, send_sem=send_sem, recv_sem=recv_sem, device_id=peer, device_id_type=MESH
        )
        copy.start()
        return copy

    for axis in range(3):
        for block in range(ns // LANES):
            row = surf_ref[axis : axis + 1, block * LANES : (block + 1) * LANES]
            surf_cols[axis, block * LANES : (block + 1) * LANES, :] = jnp.transpose(
                jnp.broadcast_to(row, (LANES, LANES))
            )

    def weigh(block, carry):
        lanes = pl.ds(pl.multiple_of(block * LANES, LANES), LANES)
        coords = [jnp.broadcast_to(vol_ref[a : a + 1, lanes], (ROWS_W, LANES)) for a in range(3)]

        def chunk(step, sums):
            rows = pl.ds(pl.multiple_of(step * ROWS_W, ROWS_W), ROWS_W)
            delta = [coords[a] - surf_cols[a, rows, :] for a in range(3)]
            dist = delta[0] * delta[0] + delta[1] * delta[1] + delta[2] * delta[2]
            near, far = dist + near_square, dist + far_square
            near = near * near
            top = (near_square * near_square) * far + (far_weight * far_square) * near
            value = top * pl.reciprocal(near * far)
            high, low = split(value)
            w_high[rows, lanes] = high
            w_low[rows, lanes] = low
            return sums + jnp.sum(value.reshape(ROWS_W // 8, 8, LANES), axis=0)

        sums = lax.fori_loop(0, ns // ROWS_W, chunk, jnp.zeros((8, LANES), jnp.float32), unroll=2)
        tot[block // 8, pl.ds(lax.rem(block, 8), 1), :] = jnp.sum(sums, axis=0, keepdims=True)
        return carry

    lax.fori_loop(0, nv // LANES, weigh, 0)

    links = links_ref[...]
    patch = jnp.bitwise_and(jnp.right_shift(links, 10) - surf + (PATCHES + 1), PATCHES - 1)
    valid = links >= 0
    idx[...] = jnp.where(valid, patch * ns + jnp.bitwise_and(links, ns - 1), -1)
    degree = jnp.sum(jnp.where(valid, 1.0, 0.0), axis=0, keepdims=True)
    diagonal = 1.0 / (1.0 + smoothing * degree)

    def count(first, last):
        def lane_block(block, carry):
            lanes = pl.ds(pl.multiple_of(block * LANES, LANES), LANES)
            wanted = [jnp.broadcast_to(idx[k : k + 1, lanes], (ROWS_A, LANES)) for k in range(idx.shape[0])]
            iota = lax.broadcasted_iota(jnp.int32, (ROWS_A, LANES), 0)

            def chunk(step, inner):
                start = pl.multiple_of(step * ROWS_A, ROWS_A)
                node = iota + start
                total = jnp.where(node == wanted[0], 1.0, 0.0)
                for k in range(1, len(wanted)):
                    total = total + jnp.where(node == wanted[k], 1.0, 0.0)
                adj[pl.ds(start, ROWS_A), lanes] = total.astype(jnp.bfloat16)
                return inner

            return lax.fori_loop(0, 3 * ns // ROWS_A, chunk, carry)

        lax.fori_loop(first, last, lane_block, 0)

    pl.semaphore_wait(barrier, len(peers))

    copies = [
        send(tot.at[lax.rem(x + d, NX)], rx.at[d - 1], sx_sem.at[d - 1], rx_sem.at[d - 1], x_peers[d - 1])
        for d in range(1, NX)
    ]
    count(0, 2)
    for copy in copies:
        copy.wait()
    zsend[...] = tot[x] + rx[0] + rx[1] + rx[2]
    order = sorted(range(1, NZ), key=lambda d: -min(d, NZ - d))
    copies = [
        send(zsend, zbuf.at[d - 1], sz_sem.at[d - 1], rz_sem.at[d - 1], z_peers[d - 1]) for d in order
    ]
    count(2, 7)
    for copy in copies:
        copy.wait()
    total = zsend[...]
    for d in range(NZ - 1):
        total = total + zbuf[d]
    inv[x] = 1.0 / total
    copies = [
        send(inv.at[x], inv.at[x], sg_sem.at[d - 1], rg_sem.at[d - 1], x_peers[d - 1]) for d in range(1, NX)
    ]
    count(7, 8)
    for copy in copies:
        copy.wait()

    rows = sens_ref.shape[0]
    for block in range(nv // LANES):
        lanes = slice(block * LANES, (block + 1) * LANES)
        high, low = split(
            sens_ref[:, lanes].astype(jnp.float32) * inv[block // 8, block % 8 : block % 8 + 1, :]
        )
        scaled[:rows, lanes] = high
        scaled[rows:, lanes] = low

    def product(step, carry):
        nodes = pl.ds(pl.multiple_of(step * 256, 256), 256)
        both = lax.dot_general(scaled[...], w_high[nodes, :], NT, preferred_element_type=jnp.float32)
        rest = lax.dot_general(scaled[:rows, :], w_low[nodes, :], NT, preferred_element_type=jnp.float32)
        prod[:, nodes] = both[:rows] + both[rows:] + rest
        return carry

    lax.fori_loop(0, ns // 256, product, 0)

    for d in range(2 * NY):
        rs[d % 2, d // 2] = prod[d * share : (d + 1) * share, :]
    copy = send(rs.at[1 - core], pr, sp_sem, rp_sem, partner)
    copy.wait()
    for d in range(NY):
        ysend[d] = rs[core, d] + pr[d]
    copies = [
        send(ysend.at[lax.rem(y + d, NY)], yr.at[d - 1], sy_sem.at[d - 1], ry_sem.at[d - 1], y_peers[d - 1])
        for d in range(1, NY)
    ]
    for copy in copies:
        copy.wait()
    source = ysend[y] + yr[0] + yr[1] + yr[2]
    cur[0] = source

    for slot in range(3):
        stage[slot] = jnp.zeros(stage.shape[1:], jnp.float32)

    def neighbours(value, part):
        stage[part, :share, :] = value
        high, low = split(stage[part])
        both = jnp.concatenate([high, low], axis=0)
        half = high.shape[0]
        result = jnp.dot(both, adj[part * ns : (part + 1) * ns, :], preferred_element_type=jnp.float32)
        return result[:share] + result[half : half + share]

    for sweep in range(SWEEPS):
        to_right = send(cur.at[sweep], halo.at[sweep, 0], sh_sem.at[sweep, 0], rh_sem.at[sweep, 0], right)
        to_left = send(cur.at[sweep], halo.at[sweep, 1], sh_sem.at[sweep, 1], rh_sem.at[sweep, 1], left)
        total = neighbours(cur[sweep], 1)
        to_right.wait()
        total = total + neighbours(halo[sweep, 0], 0)
        to_left.wait()
        total = total + neighbours(halo[sweep, 1], 2)
        result = (source + smoothing * total) * diagonal
        if sweep < SWEEPS - 1:
            cur[sweep + 1] = result
        else:
            out_ref[...] = result


def per_device(vol_coords, surf_coords, vol_sens, links):
    nv, ns, rows = vol_coords.shape[1], surf_coords.shape[1], vol_sens.shape[0]
    share = rows // (2 * NY)
    f32, bf16 = jnp.float32, jnp.bfloat16
    vmem, dma = pltpu.VMEM, pltpu.SemaphoreType.DMA
    return pl.pallas_call(
        kernel,
        out_shape=jax.ShapeDtypeStruct((share, ns), f32),
        in_specs=[pl.BlockSpec(memory_space=vmem)] * 4,
        out_specs=pl.BlockSpec(memory_space=vmem),
        scratch_shapes=[
            vmem((3, ns, LANES), f32),
            vmem((ns, nv), bf16),
            vmem((ns, nv), bf16),
            vmem((NX, 8, LANES), f32),
            vmem((NX - 1, 8, LANES), f32),
            vmem((8, LANES), f32),
            vmem((NZ - 1, 8, LANES), f32),
            vmem((NX, 8, LANES), f32),
            vmem((2 * rows, nv), bf16),
            vmem((rows, ns), f32),
            vmem((2, NY, share, ns), f32),
            vmem((NY, share, ns), f32),
            vmem((NY, share, ns), f32),
            vmem((NY - 1, share, ns), f32),
            vmem((SWEEPS, share, ns), f32),
            vmem((SWEEPS, 2, share, ns), f32),
            vmem(links.shape, jnp.int32),
            vmem((3 * ns, ns), bf16),
            vmem((3, 16, ns), f32),
            dma((NX - 1,)), dma((NX - 1,)),
            dma((NZ - 1,)), dma((NZ - 1,)),
            dma((NX - 1,)), dma((NX - 1,)),
            dma, dma,
            dma((NY - 1,)), dma((NY - 1,)),
            dma((SWEEPS, 2)), dma((SWEEPS, 2)),
        ],
        compiler_params=pltpu.CompilerParams(
            collective_id=0, has_side_effects=True, vmem_limit_bytes=52 * 2**20
        ),
    )(vol_coords, surf_coords, vol_sens, links)


def solution(mesh):
    return jax.shard_map(
        per_device,
        mesh=mesh,
        in_specs=(P(None, "vol"), P(None, "surf"), P(None, "vol"), P(None, "surf")),
        out_specs=P("vol", "surf"),
        check_vma=False,
    )
```

time: 638 us -> 79.2 us (0.12)
  the two profiles are of different devices: /device:TPU:24 before, /device:TPU:8 now
where the time goes in v1:
time: 79.2 us; the launch traced here: 78.9 us
  Pallas kernels  74.8 us (94%)
  local copies, waits for them, and re-layouts  4.08 us (5%)
    pallas_call x1, Pallas kernels, per_device(): pl.pallas_call(kernel, out_shape=jax.ShapeDtypeStruct((share, ns), f32),...  74.8 us
    unnamed x9, local copies, waits for them, and re-layouts  4.08 us

profile of v1, /device:TPU:8, one launch (start us, length us, event | category | flops | bytes accessed | tf_op | source)
XLA Modules:
  0.0 78.9 jit_solution(4553435728511426089)
XLA Ops:
  0.0 0.0 copy-start
  0.0 1.1 %copy-done = bf16[96,4096]{1,0:T(8,128)(2,1)S(1)} copy-done((bf16[96,4096]{1,0:T(8,128)(2,1)S(1)}, bf16[96,4096]{1,0:T(8,128)(2,1)}, u32[]{:S(2)}) %copy-start) | copy-done | bytes 786456
  1.1 0.0 copy-start.1
  1.1 0.8 %copy-done.1 = f32[3,4096]{1,0:T(4,128)S(1)} copy-done((f32[3,4096]{1,0:T(4,128)S(1)}, f32[3,4096]{1,0:T(4,128)}, u32[]{:S(2)}) %copy-start.1) | copy-done | bytes 49176
  2.0 0.0 copy-start.2
  2.0 0.8 copy-done.2
  2.7 0.0 copy-start.3
  2.7 0.7 copy-done.3
  3.5 74.8 %shard_map.46 = f32[12,1024]{1,0:T(8,128)S(1)} custom-call(f32[3,4096]{1,0:T(4,128)S(1)} %copy-done.1, f32[3,1024]{1,0:T(4,128)S(1)} %copy-done.3, bf16[96,4096]{1,0:T(8,128)(2,1)S(1)} %copy-done, s32[8,1024]{1,0:T(8,128)S(1)} %copy-done.2), custom_call_target="tpu_custom_call" | custom-call | tf_op jit(solution)/shard_map/pallas_call | solution.py:212
  78.3 0.6 copy.6
Async XLA Ops:
  0.0 1.1 %copy-start = (bf16[96,4096]{1,0:T(8,128)(2,1)S(1)}, bf16[96,4096]{1,0:T(8,128)(2,1)}, u32[]{:S(2)}) copy-start(bf16[96,4096]{1,0:T(8,128)(2,1)} %sens_ref.1) | copy-start | bytes 2359300
  1.1 0.8 %copy-start.1 = (f32[3,4096]{1,0:T(4,128)S(1)}, f32[3,4096]{1,0:T(4,128)}, u32[]{:S(2)}) copy-start(f32[3,4096]{1,0:T(4,128)} %vol_ref.1) | copy-start | bytes 147460
  2.0 0.8 copy-start.2
  2.7 0.7 copy-start.3

commit v2 on v1

v2 whole, which is shorter than its diff:
```python
import functools

import jax
import jax.numpy as jnp
from jax import lax
from jax.experimental import pallas as pl
from jax.experimental.pallas import tpu as pltpu
from jax.sharding import PartitionSpec as P

SWEEPS = 4
NX, NZ, NY = 4, 16, 4
PATCHES = NX * NZ
LANES = 128
MESH = pl.DeviceIdType.MESH

near_square = 0.0016
far_square = 4.0
far_weight = 0.001
smoothing = 2.0

ROWS_W = 64
ROWS_A = 128
NODES = 256
NT = (((1,), (1,)), ((), ()))


def split(value):
    high = value.astype(jnp.bfloat16)
    low = (value - high.astype(jnp.float32)).astype(jnp.bfloat16)
    return high, low


def kernel(
    vol_hbm, surf_hbm, sens_hbm, links_hbm, out_ref, vol_ref, surf_ref, sens_ref, links_ref,
    surf_cols, w_high, w_low, tot, rx, zsend, zbuf, inv, scaled, prod, rs, pr, ysend, yr,
    cur, halo, idx, adj, stage,
    sx_sem, rx_sem, sz_sem, rz_sem, sg_sem, rg_sem, sp_sem, rp_sem, sy_sem, ry_sem, sh_sem, rh_sem, in_sem,
):
    nv = vol_ref.shape[1]
    ns = surf_ref.shape[1]
    share = out_ref.shape[0]
    vol = lax.axis_index("vol")
    surf = lax.axis_index("surf")
    x, z = surf // NZ, lax.rem(surf, NZ)
    y, core = vol // 2, lax.rem(vol, 2)
    x_peers = [(vol, lax.rem(x + d, NX) * NZ + z) for d in range(1, NX)]
    z_peers = [(vol, x * NZ + lax.rem(z + d, NZ)) for d in range(1, NZ)]
    y_peers = [(lax.rem(y + d, NY) * 2 + core, surf) for d in range(1, NY)]
    partner = (y * 2 + 1 - core, surf)
    right = (vol, lax.rem(surf + 1, PATCHES))
    left = (vol, lax.rem(surf + PATCHES - 1, PATCHES))

    loads = [
        pltpu.make_async_copy(src, dst, in_sem.at[i])
        for i, (src, dst) in enumerate(
            [(surf_hbm, surf_ref), (vol_hbm, vol_ref), (links_hbm, links_ref), (sens_hbm, sens_ref)]
        )
    ]
    for load in loads:
        load.start()

    barrier = pltpu.get_barrier_semaphore()
    peers = z_peers + x_peers + y_peers + [partner, left, right]
    for peer in peers:
        pl.semaphore_signal(barrier, inc=1, device_id=peer, device_id_type=MESH)

    def send(src, dst, send_sem, recv_sem, peer):
        copy = pltpu.make_async_remote_copy(
            src_ref=src, dst_ref=dst, send_sem=send_sem, recv_sem=recv_sem, device_id=peer, device_id_type=MESH
        )
        copy.start()
        return copy

    loads[0].wait()
    for axis in range(3):
        for block in range(ns // LANES):
            row = surf_ref[axis : axis + 1, block * LANES : (block + 1) * LANES]
            surf_cols[axis, block * LANES : (block + 1) * LANES, :] = jnp.transpose(
                jnp.broadcast_to(row, (LANES, LANES))
            )

    loads[1].wait()
    piece = nv // NX

    def weigh_piece(d):
        owner = lax.rem(x + d, NX)

        def weigh(block, carry):
            source_lanes = pl.ds(pl.multiple_of(owner * piece + block * LANES, LANES), LANES)
            lanes = pl.ds(pl.multiple_of(d * piece + block * LANES, LANES), LANES)
            coords = [jnp.broadcast_to(vol_ref[a : a + 1, source_lanes], (ROWS_W, LANES)) for a in range(3)]

            def chunk(step, sums):
                rows = pl.ds(pl.multiple_of(step * ROWS_W, ROWS_W), ROWS_W)
                delta = [coords[a] - surf_cols[a, rows, :] for a in range(3)]
                dist = delta[0] * delta[0] + delta[1] * delta[1] + delta[2] * delta[2]
                near, far = dist + near_square, dist + far_square
                near = near * near
                top = (near_square * near_square) * far + (far_weight * far_square) * near
                value = top * pl.reciprocal(near * far)
                high, low = split(value)
                w_high[rows, lanes] = high
                w_low[rows, lanes] = low
                return sums + jnp.sum(value.reshape(ROWS_W // 8, 8, LANES), axis=0)

            sums = lax.fori_loop(0, ns // ROWS_W, chunk, jnp.zeros((8, LANES), jnp.float32), unroll=2)
            tot[d, pl.ds(block, 1), :] = jnp.sum(sums, axis=0, keepdims=True)
            return carry

        lax.fori_loop(0, piece // LANES, weigh, 0)

    def send_piece(d):
        return send(tot.at[d], rx.at[d - 1], sx_sem.at[d - 1], rx_sem.at[d - 1], x_peers[d - 1])

    weigh_piece(1)
    weigh_piece(2)
    pl.semaphore_wait(barrier, len(peers))
    copies = [send_piece(1), send_piece(2)]
    weigh_piece(3)
    copies.append(send_piece(3))
    weigh_piece(0)

    for copy in copies:
        copy.wait()
    zsend[...] = tot[0] + rx[0] + rx[1] + rx[2]
    order = sorted(range(1, NZ), key=lambda d: -min(d, NZ - d))
    copies = [
        send(zsend, zbuf.at[d - 1], sz_sem.at[d - 1], rz_sem.at[d - 1], z_peers[d - 1]) for d in order
    ]

    loads[2].wait()
    links = links_ref[...]
    patch = jnp.bitwise_and(jnp.right_shift(links, 10) - surf + (PATCHES + 1), PATCHES - 1)
    valid = links >= 0
    idx[...] = jnp.where(valid, patch * ns + jnp.bitwise_and(links, ns - 1), -1).astype(jnp.float32)
    degree = jnp.sum(jnp.where(valid, 1.0, 0.0), axis=0, keepdims=True)
    diagonal = 1.0 / (1.0 + smoothing * degree)

    iota = lax.broadcasted_iota(jnp.int32, (ROWS_A, LANES), 0).astype(jnp.float32).astype(jnp.bfloat16)
    one, zero = jnp.bfloat16(1.0), jnp.bfloat16(0.0)

    def lane_block(block, carry):
        lanes = pl.ds(pl.multiple_of(block * LANES, LANES), LANES)
        wanted = idx[:, lanes]

        def chunk(step, inner):
            start = pl.multiple_of(step * ROWS_A, ROWS_A)
            near = (wanted - (step * ROWS_A).astype(jnp.float32)).astype(jnp.bfloat16)
            total = None
            for k in range(idx.shape[0]):
                hit = jnp.where(iota == jnp.broadcast_to(near[k : k + 1, :], (ROWS_A, LANES)), one, zero)
                total = hit if total is None else total + hit
            adj[pl.ds(start, ROWS_A), lanes] = total
            return inner

        return lax.fori_loop(0, 3 * ns // ROWS_A, chunk, carry)

    lax.fori_loop(0, ns // LANES, lane_block, 0)
    loads[3].wait()

    for copy in copies:
        copy.wait()
    total = zsend[...]
    for d in range(NZ - 1):
        total = total + zbuf[d]
    inv[x] = 1.0 / total
    copies = [
        send(inv.at[x], inv.at[x], sg_sem.at[d - 1], rg_sem.at[d - 1], x_peers[d - 1]) for d in range(1, NX)
    ]

    rows = sens_ref.shape[0]

    def scale(d):
        owner = lax.rem(x + d, NX)
        for block in range(piece // LANES):
            source_lanes = pl.ds(pl.multiple_of(owner * piece + block * LANES, LANES), LANES)
            lanes = slice(d * piece + block * LANES, d * piece + (block + 1) * LANES)
            high, low = split(sens_ref[:, source_lanes].astype(jnp.float32) * inv[owner, block : block + 1, :])
            scaled[:rows, lanes] = high
            scaled[rows:, lanes] = low

    def product(nodes, lanes):
        both = lax.dot_general(scaled[:, lanes], w_high[nodes, lanes], NT, preferred_element_type=jnp.float32)
        rest = lax.dot_general(scaled[:rows, lanes], w_low[nodes, lanes], NT, preferred_element_type=jnp.float32)
        return both[:rows] + both[rows:] + rest

    def own_product(step, carry):
        nodes = pl.ds(pl.multiple_of(step * NODES, NODES), NODES)
        prod[step] = product(nodes, slice(0, piece))
        return carry

    scale(0)
    lax.fori_loop(0, ns // NODES, own_product, 0)
    for copy in copies:
        copy.wait()
    for d in range(1, NX):
        scale(d)

    def to_y(block, copy):
        copy.wait()
        for d in range(NY):
            ysend[block, d] = rs[block, core, d] + pr[block, d]
        return [
            send(
                ysend.at[block, lax.rem(y + d, NY)], yr.at[block, d - 1],
                sy_sem.at[block, d - 1], ry_sem.at[block, d - 1], y_peers[d - 1],
            )
            for d in range(1, NY)
        ]

    to_partner, copies = None, []
    for block in range(ns // NODES):
        prod[block] = prod[block] + product(slice(block * NODES, (block + 1) * NODES), slice(piece, nv))
        for d in range(2 * NY):
            rs[block, d % 2, d // 2] = prod[block, d * share : (d + 1) * share, :]
        copy = send(rs.at[block, 1 - core], pr.at[block], sp_sem.at[block], rp_sem.at[block], partner)
        if to_partner is not None:
            copies.append(to_y(block - 1, to_partner))
        to_partner = copy
    copies.append(to_y(ns // NODES - 1, to_partner))
    for block in range(ns // NODES):
        for copy in copies[block]:
            copy.wait()
        cur[0, :, block * NODES : (block + 1) * NODES] = (
            ysend[block, y] + yr[block, 0] + yr[block, 1] + yr[block, 2]
        )
    source = cur[0]

    for slot in range(3):
        stage[slot] = jnp.zeros(stage.shape[1:], jnp.float32)

    def neighbours(value, part):
        stage[part, :share, :] = value
        high, low = split(stage[part])
        both = jnp.concatenate([high, low], axis=0)
        half = high.shape[0]
        result = jnp.dot(both, adj[part * ns : (part + 1) * ns, :], preferred_element_type=jnp.float32)
        return result[:share] + result[half : half + share]

    for sweep in range(SWEEPS):
        to_right = send(cur.at[sweep], halo.at[sweep, 0], sh_sem.at[sweep, 0], rh_sem.at[sweep, 0], right)
        to_left = send(cur.at[sweep], halo.at[sweep, 1], sh_sem.at[sweep, 1], rh_sem.at[sweep, 1], left)
        total = neighbours(cur[sweep], 1)
        to_right.wait()
        total = total + neighbours(halo[sweep, 0], 0)
        to_left.wait()
        total = total + neighbours(halo[sweep, 1], 2)
        result = (source + smoothing * total) * diagonal
        if sweep < SWEEPS - 1:
            cur[sweep + 1] = result
        else:
            out_ref[...] = result


def per_device(vol_coords, surf_coords, vol_sens, links):
    nv, ns, rows = vol_coords.shape[1], surf_coords.shape[1], vol_sens.shape[0]
    share, blocks = rows // (2 * NY), ns // NODES
    f32, bf16 = jnp.float32, jnp.bfloat16
    vmem, dma = pltpu.VMEM, pltpu.SemaphoreType.DMA
    return pl.pallas_call(
        kernel,
        out_shape=jax.ShapeDtypeStruct((share, ns), f32),
        in_specs=[pl.BlockSpec(memory_space=pltpu.HBM)] * 4,
        out_specs=pl.BlockSpec(memory_space=vmem),
        scratch_shapes=[
            vmem(vol_coords.shape, f32),
            vmem(surf_coords.shape, f32),
            vmem(vol_sens.shape, bf16),
            vmem(links.shape, jnp.int32),
            vmem((3, ns, LANES), f32),
            vmem((ns, nv), bf16),
            vmem((ns, nv), bf16),
            vmem((NX, 8, LANES), f32),
            vmem((NX - 1, 8, LANES), f32),
            vmem((8, LANES), f32),
            vmem((NZ - 1, 8, LANES), f32),
            vmem((NX, 8, LANES), f32),
            vmem((2 * rows, nv), bf16),
            vmem((blocks, rows, NODES), f32),
            vmem((blocks, 2, NY, share, NODES), f32),
            vmem((blocks, NY, share, NODES), f32),
            vmem((blocks, NY, share, NODES), f32),
            vmem((blocks, NY - 1, share, NODES), f32),
            vmem((SWEEPS, share, ns), f32),
            vmem((SWEEPS, 2, share, ns), f32),
            vmem(links.shape, f32),
            vmem((3 * ns, ns), bf16),
            vmem((3, 16, ns), f32),
            dma((NX - 1,)), dma((NX - 1,)),
            dma((NZ - 1,)), dma((NZ - 1,)),
            dma((NX - 1,)), dma((NX - 1,)),
            dma((blocks,)), dma((blocks,)),
            dma((blocks, NY - 1)), dma((blocks, NY - 1)),
            dma((SWEEPS, 2)), dma((SWEEPS, 2)),
            dma((4,)),
        ],
        compiler_params=pltpu.CompilerParams(
            collective_id=0, has_side_effects=True, vmem_limit_bytes=67_043_328
        ),
    )(vol_coords, surf_coords, vol_sens, links)


def solution(mesh):
    return jax.shard_map(
        per_device,
        mesh=mesh,
        in_specs=(P(None, "vol"), P(None, "surf"), P(None, "vol"), P(None, "surf")),
        out_specs=P("vol", "surf"),
        check_vma=False,
    )
```

time: 79.2 us -> 73.9 us (0.933)
  local copies, waits for them, and re-layouts: 4.08 us -> 1.47 us
  Pallas kernels: 74.8 us -> 72.3 us
    unnamed x9 -> x1, local copies, waits for them, and re-layouts: 4.08 us -> 1.47 us
    pallas_call x1, Pallas kernels: 74.8 us -> 72.3 us  [per_device(): pl.pallas_call(kernel, out_shape=jax.ShapeDtypeStruct((share, ns), f32),...]
where the time goes in v2:
time: 73.9 us; the launch traced here: 73.7 us
  Pallas kernels  72.3 us (98%)
  local copies, waits for them, and re-layouts  1.47 us (2%)
    pallas_call x1, Pallas kernels, per_device(): pl.pallas_call(kernel, out_shape=jax.ShapeDtypeStruct((share, ns), f32),...  72.3 us

profile of v2, /device:TPU:8, one launch (start us, length us, event | category | flops | bytes accessed | tf_op | source)
XLA Modules:
  0.0 73.7 jit_solution(8958687463753583349)
XLA Ops:
  0.0 72.3 %shard_map.46 = f32[12,1024]{1,0:T(8,128)} custom-call(f32[3,4096]{1,0:T(4,128)} %vol_hbm.1, f32[3,1024]{1,0:T(4,128)} %surf_hbm.1, bf16[96,4096]{1,0:T(8,128)(2,1)} %sens_hbm.1, s32[8,1024]{1,0:T(8,128)} %links_hbm.1), custom_call_target="tpu_custom_call" | custom-call | tf_op jit(solution)/shard_map/pallas_call | solution.py:260
  72.3 1.5 %copy.6 = f32[12,1024]{1,0:T(8,128)} copy(f32[12,1024]{1,0:T(8,128)} %shard_map.46) | data formatting | bytes 98304

commit v3 on v2

--- a/solution.py
+++ b/solution.py
@@ -33,7 +33,7 @@
 def kernel(
     vol_hbm, surf_hbm, sens_hbm, links_hbm, out_ref, vol_ref, surf_ref, sens_ref, links_ref,
     surf_cols, w_high, w_low, tot, rx, zsend, zbuf, inv, scaled, prod, rs, pr, ysend, yr,
-    cur, halo, idx, adj, stage,
+    cur, packed, halo, idx, adj, stage,
     sx_sem, rx_sem, sz_sem, rz_sem, sg_sem, rg_sem, sp_sem, rp_sem, sy_sem, ry_sem, sh_sem, rh_sem, in_sem,
 ):
     nv = vol_ref.shape[1]
@@ -112,12 +112,10 @@
     def send_piece(d):
         return send(tot.at[d], rx.at[d - 1], sx_sem.at[d - 1], rx_sem.at[d - 1], x_peers[d - 1])
 
-    weigh_piece(1)
-    weigh_piece(2)
+    for d in range(1, NX):
+        weigh_piece(d)
     pl.semaphore_wait(barrier, len(peers))
-    copies = [send_piece(1), send_piece(2)]
-    weigh_piece(3)
-    copies.append(send_piece(3))
+    copies = [send_piece(d) for d in range(1, NX)]
     weigh_piece(0)
 
     for copy in copies:
@@ -218,38 +216,63 @@
             copies.append(to_y(block - 1, to_partner))
         to_partner = copy
     copies.append(to_y(ns // NODES - 1, to_partner))
-    for block in range(ns // NODES):
-        for copy in copies[block]:
-            copy.wait()
-        cur[0, :, block * NODES : (block + 1) * NODES] = (
-            ysend[block, y] + yr[block, 0] + yr[block, 1] + yr[block, 2]
-        )
-    source = cur[0]
-
     for slot in range(3):
         stage[slot] = jnp.zeros(stage.shape[1:], jnp.float32)
 
-    def neighbours(value, part):
-        stage[part, :share, :] = value
-        high, low = split(stage[part])
+    half = ns // 2
+    quarters = [slice(q * NODES, (q + 1) * NODES) for q in range(4)]
+
+    def send_half(sweep, part):
+        for q in range(2):
+            packed[sweep, part, q * share : (q + 1) * share, :] = stage[1, :share, quarters[2 * part + q]]
+        return [
+            send(
+                packed.at[sweep, part], halo.at[sweep, side, part],
+                sh_sem.at[sweep, side, part], rh_sem.at[sweep, side, part], peer,
+            )
+            for side, peer in enumerate((right, left))
+        ]
+
+    def neighbours(slot, nodes, columns):
+        high, low = split(stage[slot, :, nodes])
         both = jnp.concatenate([high, low], axis=0)
-        half = high.shape[0]
-        result = jnp.dot(both, adj[part * ns : (part + 1) * ns, :], preferred_element_type=jnp.float32)
-        return result[:share] + result[half : half + share]
+        rows = slice(slot * ns + nodes.start, slot * ns + nodes.stop)
+        result = jnp.dot(both, adj[rows, columns], preferred_element_type=jnp.float32)
+        return result[:share] + result[high.shape[0] : high.shape[0] + share]
+
+    halves = [slice(0, half), slice(half, ns)]
+    whole = slice(0, ns)
+    sent = []
+    for part in range(2):
+        for block in range(2 * part, 2 * part + 2):
+            for copy in copies[block]:
+                copy.wait()
+            value = ysend[block, y] + yr[block, 0] + yr[block, 1] + yr[block, 2]
+            cur[:, quarters[block]] = value
+            stage[1, :share, quarters[block]] = value
+        sent.append(send_half(0, part))
 
     for sweep in range(SWEEPS):
-        to_right = send(cur.at[sweep], halo.at[sweep, 0], sh_sem.at[sweep, 0], rh_sem.at[sweep, 0], right)
-        to_left = send(cur.at[sweep], halo.at[sweep, 1], sh_sem.at[sweep, 1], rh_sem.at[sweep, 1], left)
-        total = neighbours(cur[sweep], 1)
-        to_right.wait()
-        total = total + neighbours(halo[sweep, 0], 0)
-        to_left.wait()
-        total = total + neighbours(halo[sweep, 1], 2)
-        result = (source + smoothing * total) * diagonal
-        if sweep < SWEEPS - 1:
-            cur[sweep + 1] = result
-        else:
-            out_ref[...] = result
+        total = neighbours(1, whole, whole)
+        arriving, sent = sent, []
+        for part in range(2):
+            for side in range(2):
+                arriving[part][side].wait()
+                for q in range(2):
+                    stage[2 * side, :share, quarters[2 * part + q]] = halo[
+                        sweep, side, part, q * share : (q + 1) * share, :
+                    ]
+            if part == 0:
+                total = total + (neighbours(0, halves[0], whole) + neighbours(2, halves[0], whole))
+        for part in range(2):
+            nodes = halves[part]
+            last = neighbours(0, halves[1], nodes) + neighbours(2, halves[1], nodes)
+            result = (cur[:, nodes] + smoothing * (total[:, nodes] + last)) * diagonal[:, nodes]
+            if sweep < SWEEPS - 1:
+                stage[1, :share, nodes] = result
+                sent.append(send_half(sweep + 1, part))
+            else:
+                out_ref[:, nodes] = result
 
 
 def per_device(vol_coords, surf_coords, vol_sens, links):
@@ -281,8 +304,9 @@
             vmem((blocks, NY, share, NODES), f32),
             vmem((blocks, NY, share, NODES), f32),
             vmem((blocks, NY - 1, share, NODES), f32),
-            vmem((SWEEPS, share, ns), f32),
-            vmem((SWEEPS, 2, share, ns), f32),
+            vmem((share, ns), f32),
+            vmem((SWEEPS, 2, 2 * share, NODES), f32),
+            vmem((SWEEPS, 2, 2, 2 * share, NODES), f32),
             vmem(links.shape, f32),
             vmem((3 * ns, ns), bf16),
             vmem((3, 16, ns), f32),
@@ -291,7 +315,7 @@
             dma((NX - 1,)), dma((NX - 1,)),
             dma((blocks,)), dma((blocks,)),
             dma((blocks, NY - 1)), dma((blocks, NY - 1)),
-            dma((SWEEPS, 2)), dma((SWEEPS, 2)),
+            dma((SWEEPS, 2, 2)), dma((SWEEPS, 2, 2)),
             dma((4,)),
         ],
         compiler_params=pltpu.CompilerParams(

time: 73.9 us -> 72.2 us (0.977)
  Pallas kernels: 72.3 us -> 70.5 us
    pallas_call x1, Pallas kernels: 72.3 us -> 70.5 us  [per_device(): pl.pallas_call(kernel, out_shape=jax.ShapeDtypeStruct((share, ns), f32),...]
where the time goes in v3:
time: 72.2 us; the launch traced here: 72 us
  Pallas kernels  70.5 us (98%)
  local copies, waits for them, and re-layouts  1.47 us (2%)
    pallas_call x1, Pallas kernels, per_device(): pl.pallas_call(kernel, out_shape=jax.ShapeDtypeStruct((share, ns), f32),...  70.5 us
    unnamed x1, local copies, waits for them, and re-layouts  1.47 us

profile of v3, /device:TPU:8, one launch (start us, length us, event | category | flops | bytes accessed | tf_op | source)
XLA Modules:
  0.0 72.0 jit_solution(7617308044107221627)
XLA Ops:
  0.0 70.5 %shard_map.46 = f32[12,1024]{1,0:T(8,128)} custom-call(f32[3,4096]{1,0:T(4,128)} %vol_hbm.1, f32[3,1024]{1,0:T(4,128)} %surf_hbm.1, bf16[96,4096]{1,0:T(8,128)(2,1)} %sens_hbm.1, s32[8,1024]{1,0:T(8,128)} %links_hbm.1), custom_call_target="tpu_custom_call" | custom-call | tf_op jit(solution)/shard_map/pallas_call | solution.py:283
  70.5 1.5 %copy.6 = f32[12,1024]{1,0:T(8,128)} copy(f32[12,1024]{1,0:T(8,128)} %shard_map.46) | data formatting | bytes 98304

commit v4 on v3

--- a/solution.py
+++ b/solution.py
@@ -72,9 +72,11 @@
         return copy
 
     loads[0].wait()
+    unit = 1.0 / near_square**0.5
+    origin = [surf.astype(jnp.float32), 0.0, 0.0]
     for axis in range(3):
         for block in range(ns // LANES):
-            row = surf_ref[axis : axis + 1, block * LANES : (block + 1) * LANES]
+            row = (surf_ref[axis : axis + 1, block * LANES : (block + 1) * LANES] - origin[axis]) * unit
             surf_cols[axis, block * LANES : (block + 1) * LANES, :] = jnp.transpose(
                 jnp.broadcast_to(row, (LANES, LANES))
             )
@@ -88,15 +90,18 @@
         def weigh(block, carry):
             source_lanes = pl.ds(pl.multiple_of(owner * piece + block * LANES, LANES), LANES)
             lanes = pl.ds(pl.multiple_of(d * piece + block * LANES, LANES), LANES)
-            coords = [jnp.broadcast_to(vol_ref[a : a + 1, source_lanes], (ROWS_W, LANES)) for a in range(3)]
+            coords = [
+                jnp.broadcast_to((vol_ref[a : a + 1, source_lanes] - origin[a]) * unit, (ROWS_W, LANES))
+                for a in range(3)
+            ]
 
             def chunk(step, sums):
                 rows = pl.ds(pl.multiple_of(step * ROWS_W, ROWS_W), ROWS_W)
                 delta = [coords[a] - surf_cols[a, rows, :] for a in range(3)]
                 dist = delta[0] * delta[0] + delta[1] * delta[1] + delta[2] * delta[2]
-                near, far = dist + near_square, dist + far_square
+                near, far = dist + 1.0, dist + far_square / near_square
                 near = near * near
-                top = (near_square * near_square) * far + (far_weight * far_square) * near
+                top = far + (far_weight * far_square / near_square) * near
                 value = top * pl.reciprocal(near * far)
                 high, low = split(value)
                 w_high[rows, lanes] = high

time: 72.2 us -> 71.8 us (level)
  no operation moved by 1% of the time
where the time goes in v4:
time: 71.8 us; the launch traced here: 71.6 us
  Pallas kernels  70.2 us (98%)
  local copies, waits for them, and re-layouts  1.47 us (2%)
    pallas_call x1, Pallas kernels, per_device(): pl.pallas_call(kernel, out_shape=jax.ShapeDtypeStruct((share, ns), f32),...  70.2 us
    unnamed x1, local copies, waits for them, and re-layouts  1.47 us

profile of v4, /device:TPU:8, one launch (start us, length us, event | category | flops | bytes accessed | tf_op | source)
XLA Modules:
  0.0 71.6 jit_solution(8849394834942834209)
XLA Ops:
  0.0 70.2 %shard_map.46 = f32[12,1024]{1,0:T(8,128)} custom-call(f32[3,4096]{1,0:T(4,128)} %vol_hbm.1, f32[3,1024]{1,0:T(4,128)} %surf_hbm.1, bf16[96,4096]{1,0:T(8,128)(2,1)} %sens_hbm.1, s32[8,1024]{1,0:T(8,128)} %links_hbm.1), custom_call_target="tpu_custom_call" | custom-call | tf_op jit(solution)/shard_map/pallas_call | solution.py:288
  70.2 1.5 %copy.6 = f32[12,1024]{1,0:T(8,128)} copy(f32[12,1024]{1,0:T(8,128)} %shard_map.46) | data formatting | bytes 98304
